TPU v7x, 32 devices: a whole 2x2x4 slice. The times are simulated.
32 devices in a mesh: outer: 1, inner: 32 (over z, y, x, core).
Axes of the slice: x: 2, y: 2, z: 4, core: 2. Of those that a mesh axis runs over, the one named last changes fastest.
Arguments:
- b_leaf: float32 [8192, 64], P(('outer', 'inner')), may hold values from -6 to 6
- b_sep: float32 [256, 64], P(('outer', 'inner')), may hold values from -6 to 6
- b_root: float32 [256, 64], P(('outer', 'inner')), may hold values from -6 to 6
- leaf_linv: float32 [8192, 256], P(('outer', 'inner')), as said below
- leaf_uinv: float32 [8192, 256], P(('outer', 'inner')), as said below
- leaf_lower: float32 [8192, 256], P(('outer', 'inner')), as said below
- leaf_upper: float32 [8192, 256], P(('outer', 'inner')), as said below
- sep_rows: int32 [32, 256], P(('outer', 'inner')), may hold values from 0 to 255, as said below
- sep_linv: float32 [256, 256], P(('outer', 'inner')), as said below
- sep_uinv: float32 [256, 256], P(('outer', 'inner')), as said below
- sep_lower: float32 [256, 256], P(None, ('outer', 'inner')), as said below
- sep_upper: float32 [256, 256], P(('outer', 'inner')), as said below
- root_linv: float32 [256, 256], P(('outer', 'inner')), as said below
- root_uinv: float32 [256, 256], P(('outer', 'inner')), as said below
- basis_leaf: float32 [8192, 512], P(('outer', 'inner')), as said below
- basis_sep: float32 [256, 512], P(('outer', 'inner')), as said below
- basis_root: float32 [256, 512], P(('outer', 'inner')), as said below
- g_blocks: float32 [32768, 128], P(('outer', 'inner')), may hold values from -0.25 to 0.25
- c_blocks: float32 [32768, 128], P(('outer', 'inner')), may hold values from -0.25 to 0.25
- block_cols: int32 [64, 4], P(('outer', 'inner')), may hold values from 0 to 1
Outputs:
- v_leaf: float32 [8192, 64], P(('outer', 'inner'))
- v_sep: float32 [256, 64], P(('outer', 'inner'))
- v_root: float32 [256, 64], P(('outer', 'inner'))
- coefficients: float32 [512, 64], replicated
- reduced_g: float32 [64, 64], replicated
- reduced_c: float32 [64, 64], replicated
Inputs may be any that keep to these rules, and one draw needn't show every extreme that they name: `sep_rows`: each row holds 256 distinct numbers; every row names 0 and 255. `leaf_linv`: lower triangular in each diagonal block of the stack, nonzero diagonal. `leaf_uinv`: upper triangular in each diagonal block of the stack, nonzero diagonal. `sep_linv`: lower triangular in each block of 256 rows, nonzero diagonal. `sep_uinv`: upper triangular in each block of 256 rows, nonzero diagonal. `root_linv`: lower triangular, nonzero diagonal. `root_uinv`: upper triangular, nonzero diagonal. `leaf_lower`: entries of order one over the square root of 256. `leaf_upper`: entries of order one over the square root of 256. `sep_lower`: entries of order one over the square root of the number of its columns. `sep_upper`: entries of order one over the square root of 256. basis_leaf, basis_sep and basis_root stacked by rows form Q with Q^T Q = 8704 I up to float32 rounding. `basis_sep`: part of the stacked Q described with basis_leaf. `basis_root`: part of the stacked Q described with basis_leaf.
All inputs are finite; a program needn't handle non-finite values.
Results may differ from a plain program's by a relative error of at most 0.0003.
Values sent between devices are 32-bit elements; how exact they have to be, the bound alone decides.
No kernel may reach another device: no remote copies, remote signals or barrier semaphores. Data moves between devices by JAX's collectives and lax.ppermute only.
A program may use at most 64 MiB of HBM per device.

v0:
```python
import jax
import jax.numpy as jnp
from jax import lax
from jax.sharding import PartitionSpec as P


def matmul_exact(left, right):
    return jnp.dot(left, right, precision=lax.Precision.HIGHEST, preferred_element_type=jnp.float32)


def contract_rows(left, right):
    return lax.dot_general(
        left,
        right,
        (((0,), (0,)), ((), ())),
        precision=lax.Precision.HIGHEST,
        preferred_element_type=jnp.float32,
    )


def shards(
    b_leaf,
    b_sep,
    b_root,
    leaf_linv,
    leaf_uinv,
    leaf_lower,
    leaf_upper,
    sep_rows,
    sep_linv,
    sep_uinv,
    sep_lower,
    sep_upper,
    root_linv,
    root_uinv,
    basis_leaf,
    basis_sep,
    basis_root,
    g_blocks,
    c_blocks,
    block_cols,
):
    ports = b_leaf.shape[1]
    sep_local = b_sep.shape[0]
    root_local = b_root.shape[0]
    sep_width = sep_linv.shape[1]
    selector = (sep_rows[0][:, None] == jnp.arange(sep_width, dtype=jnp.int32)[None, :]).astype(
        jnp.float32
    )
    y_leaf = matmul_exact(leaf_linv, b_leaf)
    contrib = matmul_exact(leaf_lower, y_leaf)
    t_sep = lax.psum_scatter(
        contract_rows(selector, contrib), "inner", scatter_dimension=0, tiled=True
    )
    sep_whole = lax.all_gather(b_sep - t_sep, "inner", axis=0, tiled=True)
    y_sep = matmul_exact(sep_linv, sep_whole)
    summed = lax.psum(matmul_exact(sep_lower, y_sep), ("outer", "inner"))
    sources = lax.all_gather(b_root, ("outer", "inner"), axis=0, tiled=True)
    y_root = matmul_exact(root_linv, sources - summed)
    y_root_all = lax.all_gather(y_root, ("outer", "inner"), axis=0, tiled=True)
    x_root = matmul_exact(root_uinv, y_root_all)
    x_root_all = lax.all_gather(x_root, ("outer", "inner"), axis=0, tiled=True)
    z_sep = y_sep - matmul_exact(sep_upper, x_root_all)
    z_sep_all = lax.all_gather(z_sep, "inner", axis=0, tiled=True)
    x_sep = matmul_exact(sep_uinv, z_sep_all)
    x_sep_all = lax.all_gather(x_sep, "inner", axis=0, tiled=True)
    coupled = matmul_exact(selector, x_sep_all)
    x_leaf = matmul_exact(leaf_uinv, y_leaf - matmul_exact(leaf_upper, coupled))
    node_count = float(
        lax.axis_size("outer") * lax.axis_size("inner") * (b_leaf.shape[0] + sep_local + root_local)
    )
    pieces_x = (x_leaf, x_sep, x_root)
    pieces_q = (basis_leaf, basis_sep, basis_root)
    projected = (
        contract_rows(basis_leaf, x_leaf)
        + contract_rows(basis_sep, x_sep)
        + contract_rows(basis_root, x_root)
    )
    coefficients = lax.psum(projected, ("outer", "inner")) / node_count
    cleaned = [
        values - matmul_exact(basis, coefficients) for basis, values in zip(pieces_q, pieces_x)
    ]
    local_gram = (
        contract_rows(cleaned[0], cleaned[0])
        + contract_rows(cleaned[1], cleaned[1])
        + contract_rows(cleaned[2], cleaned[2])
    )
    gram_matrix = lax.psum(local_gram, ("outer", "inner")) / node_count
    chol_lower = jnp.linalg.cholesky(gram_matrix)
    inverse_lower = lax.linalg.triangular_solve(
        chol_lower, jnp.eye(ports, dtype=jnp.float32), left_side=True, lower=True
    )
    v_leaf = matmul_exact(cleaned[0], inverse_lower.T)
    v_sep = matmul_exact(cleaned[1], inverse_lower.T)
    v_root = matmul_exact(cleaned[2], inverse_lower.T)
    block_rows = block_cols.shape[0]
    stored = block_cols.shape[1]
    block_size = g_blocks.shape[1]
    blocked = v_leaf.reshape(block_rows, block_size, ports)
    picked = blocked[block_cols]
    g_tiles = g_blocks.reshape(block_rows, stored, block_size, block_size)
    c_tiles = c_blocks.reshape(block_rows, stored, block_size, block_size)
    g_image = jnp.einsum("rwij,rwjp->rip", g_tiles, picked, precision=lax.Precision.HIGHEST)
    c_image = jnp.einsum("rwij,rwjp->rip", c_tiles, picked, precision=lax.Precision.HIGHEST)
    g_local = jnp.einsum("rip,riq->pq", blocked, g_image, precision=lax.Precision.HIGHEST)
    c_local = jnp.einsum("rip,riq->pq", blocked, c_image, precision=lax.Precision.HIGHEST)
    g_summed, c_summed = lax.psum((g_local, c_local), ("outer", "inner"))
    return (v_leaf, v_sep, v_root, coefficients, g_summed / node_count, c_summed / node_count)


def solution(mesh):
    return jax.shard_map(
        shards,
        mesh=mesh,
        in_specs=(
            P(("outer", "inner"), None),
            P(("outer", "inner"), None),
            P(("outer", "inner"), None),
            P(("outer", "inner"), None),
            P(("outer", "inner"), None),
            P(("outer", "inner"), None),
            P(("outer", "inner"), None),
            P(("outer", "inner"), None),
            P(("outer", "inner"), None),
            P(("outer", "inner"), None),
            P(None, ("outer", "inner")),
            P(("outer", "inner"), None),
            P(("outer", "inner"), None),
            P(("outer", "inner"), None),
            P(("outer", "inner"), None),
            P(("outer", "inner"), None),
            P(("outer", "inner"), None),
            P(("outer", "inner"), None),
            P(("outer", "inner"), None),
            P(("outer", "inner"), None),
        ),
        out_specs=(
            P(("outer", "inner"), None),
            P(("outer", "inner"), None),
            P(("outer", "inner"), None),
            P(),
            P(),
            P(),
        ),
        check_vma=False,
    )
```

profile of v0, /device:TPU:0, one launch (start us, length us, event | category | flops | bytes accessed | tf_op | source)
XLA Modules:
  0.0 685.7 jit_solution(16916968704119471954)
XLA Ops:
  7.2 1.4 fusion.17
  9.0 0.7 copy-done.16
  9.7 1.0 fusion.8
  10.8 130.4 %all-reduce.10.cloned.1.call-done = f32[256,64]{1,0:T(8,128)} async-done(((f32[256,64]{1,0:T(8,128)}), f32[256,64]{1,0:T(8,128)}) %all-reduce.10.cloned.1.call-update) | async-done | bytes 65552
  141.3 0.7 dynamic-slice_subtract_fusion
  142.0 40.0 %all_gather.18 = f32[256,64]{1,0:T(8,128)S(1)} all-gather(f32[8,64]{1,0:T(8,128)S(1)} %dynamic-slice_subtract_fusion), channel_id=1, replica_groups=mesh['outer'=1,'inner'=32] {'inner'}, dimensions={0}, use_global_device_ids=true | all-gather | bytes 67584 | tf_op jit(solution)/shard_map/all_gather | solution.py:55
  182.7 0.9 convolution_bitcast_fusion.3
  183.7 0.6 copy-done.19
  184.3 37.0 %all_gather.19 = f32[256,64]{1,0:T(8,128)S(1)} all-gather(f32[8,64]{1,0:T(8,128)S(1)} %copy-done.18), channel_id=1, replica_groups=mesh['outer'=1,'inner'=32] {'outer','inner'}, dimensions={0}, use_global_device_ids=true | all-gather | bytes 67584 | tf_op jit(solution)/shard_map/all_gather | solution.py:58
  221.4 77.8 %all-reduce.6.cloned.1.call-done = f32[256,64]{0,1:T(8,128)} async-done(((f32[256,64]{0,1:T(8,128)}), f32[256,64]{0,1:T(8,128)}) %all-reduce.6.cloned.1.call-update) | async-done | bytes 65552 | tf_op jit(solution)/shard_map/psum | solution.py:57
  299.2 1.0 convolution_bitcast_fusion.8
  300.2 40.4 %all_gather.20 = f32[256,64]{1,0:T(8,128)S(1)} all-gather(f32[8,64]{1,0:T(8,128)S(1)} %convolution_bitcast_fusion.8), channel_id=1, replica_groups=mesh['outer'=1,'inner'=32] {'outer','inner'}, dimensions={0}, use_global_device_ids=true | all-gather | bytes 67584 | tf_op jit(solution)/shard_map/all_gather | solution.py:60
  340.8 37.0 %all_gather.21 = f32[256,64]{1,0:T(8,128)S(1)} all-gather(f32[8,64]{1,0:T(8,128)S(1)} %bitcast.119), channel_id=1, replica_groups=mesh['outer'=1,'inner'=32] {'outer','inner'}, dimensions={0}, use_global_device_ids=true | all-gather | bytes 67584 | tf_op jit(solution)/shard_map/all_gather | solution.py:62
  377.9 38.3 %all_gather.22 = f32[256,64]{1,0:T(8,128)S(1)} all-gather(f32[8,64]{1,0:T(8,128)S(1)} %fusion.5), channel_id=1, replica_groups=mesh['outer'=1,'inner'=32] {'inner'}, dimensions={0}, use_global_device_ids=true | all-gather | bytes 67584 | tf_op jit(solution)/shard_map/all_gather | solution.py:64
  416.4 37.0 %all_gather.23 = f32[256,64]{1,0:T(8,128)S(1)} all-gather(f32[8,64]{1,0:T(8,128)S(1)} %bitcast.120), channel_id=1, replica_groups=mesh['outer'=1,'inner'=32] {'inner'}, dimensions={0}, use_global_device_ids=true | all-gather | bytes 67584 | tf_op jit(solution)/shard_map/all_gather | solution.py:66
  455.2 1.1 fusion.1
  456.4 122.1 %all-reduce.8.cloned.1.call-done = f32[512,64]{0,1:T(8,128)} async-done(((f32[512,64]{0,1:T(8,128)}), f32[512,64]{0,1:T(8,128)}) %all-reduce.8.cloned.1.call-update) | async-done | bytes 131088 | tf_op jit(solution)/shard_map/psum | solution.py:79
  578.5 0.9 broadcast_multiply_fusion
  579.4 0.6 convolution_subtract_fusion
  581.2 39.4 %psum.37 = f32[64,64]{0,1:T(8,128)S(1)} all-reduce(f32[64,64]{0,1:T(8,128)S(1)} %convolution_add_fusion.1), channel_id=1, replica_groups=mesh['outer'=1,'inner'=32] {'outer','inner'}, use_global_device_ids=true, to_apply=%region_3.0 | all-reduce | flops 4096 | bytes 32768 | tf_op jit(solution)/shard_map/psum | solution.py:88
  620.7 5.8 cholesky.17
  626.6 0.6 compare_reduce_fusion
  627.2 0.7 fusion.13
  627.9 4.9 custom-call.6
  633.3 0.8 fusion.27
  634.0 0.8 fusion.28
  634.8 0.6 gather_fusion
  635.4 0.7 convolution_bitcast_fusion.1
  636.4 0.7 convolution_bitcast_fusion
  637.3 40.4 %all-reduce.1 = (f32[64,64]{0,1:T(8,128)S(1)}, f32[64,64]{0,1:T(8,128)S(1)}) all-reduce(f32[64,64]{0,1:T(8,128)S(1)} %convolution_bitcast_fusion.5, f32[64,64]{0,1:T(8,128)S(1)} %convolution_bitcast_fusion.4), channel_id=1, replica_groups=mesh['outer'=1,'inner'=32] {'outer','inner'}, use_global_device_ids=true, to_apply=%region_6.7 | all-reduce | flops 8192 | bytes 65536 | tf_op jit(solution)/shard_map/psum | solution.py:107
  677.7 0.7 copy.69
  678.4 0.7 copy.70
  (73 shorter events, 6.0 us)
Async XLA Ops:
  7.2 628.2 %copy-start = (f32[1024,128]{1,0:T(8,128)S(1)}, f32[1024,128]{1,0:T(8,128)}, u32[]{:S(2)}) copy-start(f32[1024,128]{1,0:T(8,128)} %param.37) | copy-start | bytes 1572868
  7.2 1.5 copy-start.6
  7.2 134.1 %all-reduce.10.cloned.1.call-start = ((), (), s32[]{:S(2)}) async-start(), calls=%async_computation.2 | async-start | bytes 262144
  9.0 0.7 copy-start.16
  10.8 288.5 %all-reduce.6.cloned.1.call-start = ((), (), s32[]{:S(2)}) async-start(), calls=%async_computation | async-start | bytes 131072 | tf_op jit(solution)/shard_map/psum | solution.py:57
  10.8 130.5 %copy-start.17 = (f32[8,64]{1,0:T(8,128)S(1)}, f32[8,64]{1,0:T(8,128)}, u32[]{:S(2)}) copy-start(f32[8,64]{1,0:T(8,128)} %param.21) | copy-start | bytes 6148
  142.0 40.0 %copy-start.10 = (f32[8,256]{1,0:T(8,128)S(1)}, f32[8,256]{1,0:T(8,128)}, u32[]{:S(2)}) copy-start(f32[8,256]{1,0:T(8,128)} %param.28) | copy-start | bytes 24580
  182.0 0.7 copy-start.11
  183.6 0.7 copy-start.19
  183.6 0.7 copy-start.18
  183.6 394.9 %all-reduce.8.cloned.1.call-start = ((), (), s32[]{:S(2)}) async-start(), calls=%async_computation.1 | async-start | bytes 262144 | tf_op jit(solution)/shard_map/psum | solution.py:79
  221.3 78.0 %copy-start.12 = (f32[8,256]{1,0:T(8,128)S(1)}, f32[8,256]{1,0:T(8,128)}, u32[]{:S(2)}) copy-start(f32[8,256]{1,0:T(8,128)} %param.32) | copy-start | bytes 24580
  300.2 40.4 %copy-start.13 = (f32[8,256]{1,0:T(8,128)S(1)}, f32[8,256]{1,0:T(8,128)}, u32[]{:S(2)}) copy-start(f32[8,256]{1,0:T(8,128)} %param.33) | copy-start | bytes 24580
  340.8 37.0 %copy-start.14 = (f32[8,256]{1,0:T(8,128)S(1)}, f32[8,256]{1,0:T(8,128)}, u32[]{:S(2)}) copy-start(f32[8,256]{1,0:T(8,128)} %param.31) | copy-start | bytes 24580
  377.9 38.3 %copy-start.15 = (f32[8,256]{1,0:T(8,128)S(1)}, f32[8,256]{1,0:T(8,128)}, u32[]{:S(2)}) copy-start(f32[8,256]{1,0:T(8,128)} %param.29) | copy-start | bytes 24580
  416.4 37.3 %copy-start.9 = (f32[8,512]{1,0:T(8,128)S(1)}, f32[8,512]{1,0:T(8,128)}, u32[]{:S(2)}) copy-start(f32[8,512]{1,0:T(8,128)} %param.36) | copy-start | bytes 49156
  453.4 0.7 copy-start.8
  453.4 1.0 copy-start.5
  453.8 1.1 copy-start.7
  454.1 1.1 copy-start.1
  579.4 0.8 copy-start.2
  633.2 3.8 copy-start.3
  635.4 1.0 copy-start.4
Sparse Core Ops, SparseCore 0:
  14.1 127.1 all-reduce.9
  183.7 115.4 all-reduce.5
  456.5 121.9 all-reduce.7
where the time goes:
time: 686 us
  waiting for transfers between devices  330 us (48%)
  blocking collectives  309 us (45%)
  between operations  14.1 us (2%)
  other arithmetic  13.7 us (2%)
  matrix products  13.6 us (2%)
    unnamed x4, waiting for transfers between devices  130 us
    psum x1, waiting for transfers between devices, shards(): coefficients = lax.psum(projected, ('outer', 'inner')) / node_count  122 us
    psum x1, waiting for transfers between devices, shards(): summed = lax.psum(matmul_exact(sep_lower, y_sep), ('outer', 'inner'))  77.8 us
    psum x1, blocking collectives, shards(): g_summed, c_summed = lax.psum((g_local, c_local), ('outer', 'inner'))  40.4 us
    all_gather x1, blocking collectives, shards(): y_root_all = lax.all_gather(y_root, ('outer', 'inner'), axis=0, tiled=True)  40.4 us
    all_gather x1, blocking collectives, shards(): sep_whole = lax.all_gather(b_sep - t_sep, 'inner', axis=0, tiled=True)  40 us
    psum x1, blocking collectives, shards(): gram_matrix = lax.psum(local_gram, ('outer', 'inner')) / node_count  39.4 us
    all_gather x1, blocking collectives, shards(): z_sep_all = lax.all_gather(z_sep, 'inner', axis=0, tiled=True)  38.3 us
  transfers between devices with their start and end apart: 3, of which 3 were waited for; matrix products, arithmetic and copies ran while one was open for 0% of the time, Pallas kernels for 0%

commit v1 on v0

--- a/solution.py
+++ b/solution.py
@@ -76,7 +76,7 @@
         + contract_rows(basis_sep, x_sep)
         + contract_rows(basis_root, x_root)
     )
-    coefficients = lax.psum(projected, ("outer", "inner")) / node_count
+    coefficients = jnp.sum(lax.all_gather(projected, ("outer", "inner")), axis=0) / node_count
     cleaned = [
         values - matmul_exact(basis, coefficients) for basis, values in zip(pieces_q, pieces_x)
     ]

time: 686 us -> 635 us (0.926)
  waiting for transfers between devices: 330 us -> 267 us
  matrix products: 13.6 us -> 22.7 us
    psum x1 -> x0, waiting for transfers between devices: 122 us -> none  [shards(): coefficients = lax.psum(projected, ('outer', 'inner')) / node_count]
    all_gather x0 -> x1, waiting for transfers between devices: none -> 59.2 us  [shards(): lax.all_gather(projected, ('outer', 'inner'))]
    dot_general x17, matrix products: 8.18 us -> 15.2 us  [matmul_exact(): jnp.dot(left, right, precision=lax.Precision.HIGHEST, preferred_element_t...]
where the time goes in v1:
time: 635 us; the launch traced here: 634 us
  blocking collectives  310 us (49%)
  waiting for transfers between devices  267 us (42%)
  matrix products  22.7 us (4%)
  between operations  14 us (2%)
  other arithmetic  13.5 us (2%)
  local copies, waits for them, and re-layouts  6.81 us (1%)
    unnamed x4, waiting for transfers between devices  130 us
    psum x1, waiting for transfers between devices, shards(): summed = lax.psum(matmul_exact(sep_lower, y_sep), ('outer', 'inner'))  78.2 us
    all_gather x1, waiting for transfers between devices, shards(): lax.all_gather(projected, ('outer', 'inner'))  59.2 us
    psum x1, blocking collectives, shards(): g_summed, c_summed = lax.psum((g_local, c_local), ('outer', 'inner'))  40.4 us
    all_gather x1, blocking collectives, shards(): y_root_all = lax.all_gather(y_root, ('outer', 'inner'), axis=0, tiled=True)  40.2 us
    all_gather x1, blocking collectives, shards(): sep_whole = lax.all_gather(b_sep - t_sep, 'inner', axis=0, tiled=True)  39.9 us
    psum x1, blocking collectives, shards(): gram_matrix = lax.psum(local_gram, ('outer', 'inner')) / node_count  39.6 us
    all_gather x1, blocking collectives, shards(): z_sep_all = lax.all_gather(z_sep, 'inner', axis=0, tiled=True)  38.3 us
  transfers between devices with their start and end apart: 3, of which 3 were waited for; matrix products, arithmetic and copies ran while one was open for 0% of the time, Pallas kernels for 0%

profile of v1, /device:TPU:0, one launch (start us, length us, event | category | flops | bytes accessed | tf_op | source)
XLA Modules:
  0.0 633.8 jit_solution(4248371004321635002)
XLA Ops:
  7.2 1.4 fusion.17
  8.6 1.3 fusion.18
  10.0 1.7 fusion.8
  11.8 129.5 %all-reduce.7.cloned.1.call-done = f32[256,64]{1,0:T(8,128)} async-done(((f32[256,64]{1,0:T(8,128)}), f32[256,64]{1,0:T(8,128)}) %all-reduce.7.cloned.1.call-update) | async-done | bytes 65552
  141.3 0.7 dynamic-slice_subtract_fusion
  142.0 39.9 %all_gather.24 = f32[256,64]{1,0:T(8,128)S(1)} all-gather(f32[8,64]{1,0:T(8,128)S(1)} %dynamic-slice_subtract_fusion), channel_id=1, replica_groups=mesh['outer'=1,'inner'=32] {'inner'}, dimensions={0}, use_global_device_ids=true | all-gather | bytes 67584 | tf_op jit(solution)/shard_map/all_gather | solution.py:55
  181.9 0.9 fusion.19
  182.8 1.6 convolution_bitcast_fusion.3
  184.4 37.2 %all_gather.25 = f32[256,64]{1,0:T(8,128)S(1)} all-gather(f32[8,64]{1,0:T(8,128)} %param.22), channel_id=1, replica_groups=mesh['outer'=1,'inner'=32] {'outer','inner'}, dimensions={0}, use_global_device_ids=true | all-gather | bytes 67584 | tf_op jit(solution)/shard_map/all_gather | solution.py:58
  221.8 78.2 %all-reduce.5.cloned.1.call-done = f32[256,64]{0,1:T(8,128)} async-done(((f32[256,64]{0,1:T(8,128)}), f32[256,64]{0,1:T(8,128)}) %all-reduce.5.cloned.1.call-update) | async-done | bytes 65552 | tf_op jit(solution)/shard_map/psum | solution.py:57
  300.0 1.0 convolution_bitcast_fusion.8
  301.0 40.2 %all_gather.26 = f32[256,64]{1,0:T(8,128)S(1)} all-gather(f32[8,64]{1,0:T(8,128)S(1)} %convolution_bitcast_fusion.8), channel_id=1, replica_groups=mesh['outer'=1,'inner'=32] {'outer','inner'}, dimensions={0}, use_global_device_ids=true | all-gather | bytes 67584 | tf_op jit(solution)/shard_map/all_gather | solution.py:60
  341.2 0.9 fusion.20
  342.1 37.0 %all_gather.27 = f32[256,64]{1,0:T(8,128)S(1)} all-gather(f32[8,64]{1,0:T(8,128)S(1)} %bitcast.125), channel_id=1, replica_groups=mesh['outer'=1,'inner'=32] {'outer','inner'}, dimensions={0}, use_global_device_ids=true | all-gather | bytes 67584 | tf_op jit(solution)/shard_map/all_gather | solution.py:62
  379.0 0.9 fusion.5
  379.9 38.3 %all_gather.28 = f32[256,64]{1,0:T(8,128)S(1)} all-gather(f32[8,64]{1,0:T(8,128)S(1)} %fusion.5), channel_id=1, replica_groups=mesh['outer'=1,'inner'=32] {'inner'}, dimensions={0}, use_global_device_ids=true | all-gather | bytes 67584 | tf_op jit(solution)/shard_map/all_gather | solution.py:64
  418.2 0.9 fusion.21
  419.1 37.0 %all_gather.29 = f32[256,64]{1,0:T(8,128)S(1)} all-gather(f32[8,64]{1,0:T(8,128)S(1)} %bitcast.126), channel_id=1, replica_groups=mesh['outer'=1,'inner'=32] {'inner'}, dimensions={0}, use_global_device_ids=true | all-gather | bytes 67584 | tf_op jit(solution)/shard_map/all_gather | solution.py:66
  456.1 1.0 fusion.6
  457.1 1.0 fusion.23
  458.2 1.0 fusion.24
  459.2 1.3 fusion.2
  460.5 1.3 fusion.22
  461.9 1.1 fusion.1
  463.1 59.2 %all-gather.3.cloned.1.call-done = f32[16384,64]{0,1:T(8,128)} async-done(((f32[512,64]{0,1:T(8,128)}), f32[16384,64]{0,1:T(8,128)}) %all-gather.3.cloned.1.call-update) | async-done | bytes 4194320 | tf_op jit(solution)/shard_map/all_gather | solution.py:79
  522.3 4.6 copy.81
  529.4 39.6 %psum.29 = f32[64,64]{0,1:T(8,128)S(1)} all-reduce(f32[64,64]{0,1:T(8,128)S(1)} %convolution_add_fusion.1), channel_id=1, replica_groups=mesh['outer'=1,'inner'=32] {'outer','inner'}, use_global_device_ids=true, to_apply=%region_3.0 | all-reduce | flops 4096 | bytes 32768 | tf_op jit(solution)/shard_map/psum | solution.py:88
  569.1 5.8 cholesky.17
  576.3 4.9 custom-call.6
  581.6 0.8 fusion.28
  582.4 0.8 fusion.27
  585.5 40.4 %all-reduce.1 = (f32[64,64]{0,1:T(8,128)S(1)}, f32[64,64]{0,1:T(8,128)S(1)}) all-reduce(f32[64,64]{0,1:T(8,128)S(1)} %convolution_bitcast_fusion.5, f32[64,64]{0,1:T(8,128)S(1)} %convolution_bitcast_fusion.4), channel_id=1, replica_groups=mesh['outer'=1,'inner'=32] {'outer','inner'}, use_global_device_ids=true, to_apply=%region_6.7 | all-reduce | flops 8192 | bytes 65536 | tf_op jit(solution)/shard_map/psum | solution.py:107
  (51 shorter events, 8.4 us)
Async XLA Ops:
  7.2 576.6 %copy-start = (f32[1024,128]{1,0:T(8,128)S(1)}, f32[1024,128]{1,0:T(8,128)}, u32[]{:S(2)}) copy-start(f32[1024,128]{1,0:T(8,128)} %param.38) | copy-start | bytes 1572868
  7.2 454.7 %copy-start.1 = (f32[256,512]{1,0:T(8,128)S(1)}, f32[256,512]{1,0:T(8,128)}, u32[]{:S(2)}) copy-start(f32[256,512]{1,0:T(8,128)} %param.34) | copy-start | bytes 1572868
  7.2 455.8 %copy-start.7 = (s32[2,4]{1,0:T(2,128)S(1)}, s32[2,4]{1,0:T(2,128)}, u32[]{:S(2)}) copy-start(s32[2,4]{1,0:T(2,128)} %param.39) | copy-start | bytes 100
  7.2 134.1 %all-reduce.7.cloned.1.call-start = ((), (), s32[]{:S(2)}) async-start(), calls=%async_computation.2 | async-start | bytes 262144
  11.7 288.3 %all-reduce.5.cloned.1.call-start = ((), (), s32[]{:S(2)}) async-start(), calls=%async_computation | async-start | bytes 131072 | tf_op jit(solution)/shard_map/psum | solution.py:57
  184.4 337.9 %all-gather.3.cloned.1.call-start = ((), (), s32[]{:S(2)}) async-start(), calls=%async_computation.1 | async-start | bytes 4325376 | tf_op jit(solution)/shard_map/all_gather | solution.py:79
  526.8 1.4 copy-start.5
  526.9 1.5 copy-start.6
  526.9 57.7 %copy-start.4 = (f32[1024,128]{1,0:T(8,128)S(1)}, f32[1024,128]{1,0:T(8,128)}, u32[]{:S(2)}) copy-start(f32[1024,128]{1,0:T(8,128)} %param.37) | copy-start | bytes 1572868
  527.6 99.7 %copy-start.2 = (f32[512,64]{0,1:T(8,128)}, f32[512,64]{0,1:T(8,128)S(1)}, u32[]{:S(2)}) copy-start(f32[512,64]{0,1:T(8,128)S(1)} %broadcast_multiply_fusion) | copy-start | bytes 393220
  581.6 45.7 %copy-start.3 = (f32[256,64]{0,1:T(8,128)}, f32[256,64]{0,1:T(8,128)S(1)}, u32[]{:S(2)}) copy-start(f32[256,64]{0,1:T(8,128)S(1)} %fusion.26) | copy-start | bytes 196612
Sparse Core Ops, SparseCore 0:
  14.1 127.1 all-reduce.6
  184.5 115.4 all-reduce.4
  463.1 59.1 all-gather.2
